TPU v7x, 32 devices: a whole 2x2x4 slice. The times are simulated.
32 devices in a mesh: dom: 8 (over z, x), blk: 4 (over y, core).
Axes of the slice: x: 2, y: 2, z: 4, core: 2. Of those that a mesh axis runs over, the one named last changes fastest.
Arguments:
- multipliers: float32 [4, 48, 64, 256], P('blk', 'dom'), may hold values from -6 to 6
- residual: float32 [4, 48, 64, 256], P('blk', 'dom')
- dir_prev: float32 [4, 48, 64, 256], P('blk', 'dom'), may hold values from -6 to 6
- rho_prev: float32 [64], replicated, may hold values from 10 to 100
- face_ids: int32 [4, 16, 6], P('blk'), may hold values from 0 to 47, as said below
- face_sign: int32 [4, 16, 6], P('blk'), may hold values from -1 to 1, as said below
- dual_blocks: bfloat16 [4, 16, 1536, 1536], P('blk', 'dom'), as said below
- dirichlet_blocks: bfloat16 [4, 16, 1536, 1536], P('blk', 'dom'), as said below
- coupling: bfloat16 [4, 16, 256, 1536], P('blk', 'dom'), may hold values from -0.15625 to 0.15625
- corner_ids: int32 [4, 16, 256], P('blk', 'dom'), may hold values from 0 to 3071, as said below
- coarse_inv: bfloat16 [8, 4, 768, 768], P('dom', 'blk'), as said below
Outputs:
- new_multipliers: float32 [4, 48, 64, 256], P('blk', 'dom')
- new_residual: float32 [4, 48, 64, 256], P('blk', 'dom')
- direction: float32 [4, 48, 64, 256], P('blk', 'dom')
- rho_now: float32 [64], replicated
- reduction: float32 [64], replicated
Inputs may be any that keep to these rules, and one draw needn't show every extreme that they name: `face_ids`: in each column b every face index below 48 is named by exactly two slots, of subdomains held by two different indices of dom; face f is owned by dom index f // 6. The 2 subdomains of one dom index name at most 3 faces of any one owner, and in every column some pairs of a dom index and an owner reach 3. `face_sign`: of the two slots that name one face, one has +1 and the other -1. `dual_blocks`: each block is symmetric positive definite. `dirichlet_blocks`: each block is symmetric positive definite. `coarse_inv`: each block is symmetric positive definite. `corner_ids`: the corners of one subdomain are distinct, and corner k lies in coarse block k // 64, that is, its index n satisfies n // 768 = k // 64.
All inputs are finite; a program needn't handle non-finite values.
Results may differ from a plain program's by a relative error of at most 0.033.
Values may be sent and summed in bfloat16 or wider, within the bound.
A program may use at most 128 MiB of HBM per device.

v0:
```python
import jax
import jax.numpy as jnp
from jax import lax
from jax.sharding import PartitionSpec as P


def block_product(pieces, matrices):
    sub_count, face_slots, case_count, face_len = pieces.shape
    blocks = matrices.reshape(sub_count, face_slots, face_len, matrices.shape[-1])
    return jnp.einsum("stcx,stxm->scm", pieces, blocks, preferred_element_type=jnp.float32)


def corner_products(pieces, coupling_rows):
    sub_count, face_slots, case_count, face_len = pieces.shape
    blocks = coupling_rows.reshape(sub_count, coupling_rows.shape[1], face_slots, face_len)
    return jnp.einsum("stcx,sktx->sck", pieces, blocks, preferred_element_type=jnp.float32)


def on_device(
    multipliers,
    residual,
    dir_prev,
    rho_prev,
    face_ids,
    face_sign,
    dual_blocks,
    dirichlet_blocks,
    coupling,
    corner_ids,
    coarse_inv,
):
    n_dom = lax.axis_size("dom")
    n_blk = lax.axis_size("blk")
    my_index = lax.axis_index("dom")
    faces_dev = multipliers.shape[1]
    case_count = multipliers.shape[2]
    face_len = multipliers.shape[3]
    sub_count = dual_blocks.shape[1]
    face_slots = face_ids.shape[2]
    slot_count = sub_count * face_slots
    column_ids = face_ids[0].reshape(n_dom, slot_count)
    column_sign = face_sign[0].reshape(n_dom, slot_count)
    my_sign = lax.dynamic_index_in_dim(column_sign, my_index, 0, keepdims=False).astype(
        jnp.bfloat16
    )
    capacity = (slot_count + n_dom - 1) // n_dom + 1
    owners = column_ids // faces_dev
    slot_order = jnp.arange(slot_count)
    earlier = (owners[:, :, None] == owners[:, None, :]) & (
        slot_order[None, None, :] < slot_order[None, :, None]
    )
    slot_rank = jnp.sum(earlier.astype(jnp.int32), axis=2)
    places = jnp.arange(capacity)
    peer_index = jnp.arange(n_dom)
    face_index = jnp.arange(faces_dev)
    owned_here = (owners == my_index)[:, :, None, None]
    rank_match = slot_rank[:, :, None, None] == places[None, None, :, None]
    face_match = (column_ids % faces_dev)[:, :, None, None] == face_index[None, None, None, :]
    send_table = jnp.sum((owned_here & rank_match & face_match).astype(jnp.int32), axis=1).astype(
        jnp.bfloat16
    )
    my_owner = lax.dynamic_index_in_dim(owners, my_index, 0, keepdims=False)
    my_rank = lax.dynamic_index_in_dim(slot_rank, my_index, 0, keepdims=False)
    pull_match = (my_owner[:, None, None] == peer_index[None, :, None]) & (
        my_rank[:, None, None] == places[None, None, :]
    )
    pull_table = (pull_match.astype(jnp.bfloat16) * my_sign[:, None, None]).reshape(
        sub_count, face_slots, n_dom, capacity
    )

    def fetch_multiply(vector_half, matrices, with_coarse):

        def finish(pieces):
            product = block_product(pieces, matrices)
            if with_coarse:
                return (product, corner_products(pieces, coupling[0]))
            return product

        outgoing = jnp.einsum(
            "dkf,fcx->dkcx", send_table, vector_half, preferred_element_type=jnp.float32
        ).astype(jnp.bfloat16)
        pieces = jnp.einsum(
            "stok,okcx->stcx",
            pull_table,
            lax.all_to_all(outgoing, "dom", split_axis=0, concat_axis=0, tiled=True),
            preferred_element_type=jnp.float32,
        ).astype(jnp.bfloat16)
        return finish(pieces)

    def return_sums(totals):
        per_slot = totals.reshape(sub_count, case_count, face_slots, face_len).astype(jnp.bfloat16)
        outgoing = jnp.einsum(
            "stok,sctx->okcx", pull_table, per_slot, preferred_element_type=jnp.float32
        ).astype(jnp.bfloat16)
        incoming = lax.all_to_all(outgoing, "dom", split_axis=0, concat_axis=0, tiled=True)
        summed = jnp.einsum(
            "dkf,dkcx->fcx", send_table, incoming, preferred_element_type=jnp.float32
        )
        return summed

    def global_sums(parts):
        return lax.psum(parts, ("dom", "blk"))

    total_count = n_dom * n_blk * faces_dev * face_len
    residual_rows = residual[0]
    precond_res = return_sums(
        fetch_multiply(residual_rows.astype(jnp.bfloat16), dirichlet_blocks[0], False)
    )
    rho_sum, square_sum = global_sums(
        (
            jnp.sum(residual_rows * precond_res, axis=(0, 2)),
            jnp.sum(residual_rows * residual_rows, axis=(0, 2)),
        )
    )
    rho_now = rho_sum / total_count
    res_mean = square_sum / total_count
    beta_ratio = rho_now / rho_prev
    direction = precond_res + beta_ratio[None, :, None] * dir_prev[0]
    product, corner_terms = fetch_multiply(direction.astype(jnp.bfloat16), dual_blocks[0], True)
    corner_count = corner_terms.shape[2]
    block_span = coarse_inv.shape[2]
    coarse_span = block_span * n_blk
    flat_ids = corner_ids[0].reshape(-1)
    values = jnp.transpose(corner_terms, (1, 0, 2)).reshape(case_count, sub_count * corner_count)
    local_sums = jnp.zeros((case_count, coarse_span), jnp.float32).at[:, flat_ids].add(values)
    owned_sums = lax.psum_scatter(
        local_sums.astype(jnp.bfloat16), "blk", scatter_dimension=1, tiled=True
    )
    solved = jnp.dot(owned_sums, coarse_inv[0, 0], preferred_element_type=jnp.float32).astype(
        jnp.bfloat16
    )
    everywhere = lax.all_gather(solved, "blk", axis=1, tiled=True)
    picked = jnp.take(everywhere, flat_ids, axis=1).reshape(case_count, sub_count, corner_count)
    image_vec = return_sums(
        product
        + jnp.einsum("csk,skl->scl", picked, coupling[0], preferred_element_type=jnp.float32)
    )
    curve_local = jnp.sum(direction * image_vec, axis=(0, 2))
    (curve_sum,) = global_sums((curve_local,))
    alpha_step = rho_now / (curve_sum / total_count)
    new_res = residual_rows - alpha_step[None, :, None] * image_vec
    (new_sum,) = global_sums((jnp.sum(new_res * new_res, axis=(0, 2)),))
    reduction = new_sum / total_count / res_mean
    new_lam = multipliers[0] + alpha_step[None, :, None] * direction
    return (new_lam[None], new_res[None], direction[None], rho_now, reduction)


def solution(mesh):
    in_specs = (
        P("blk", "dom", None, None),
        P("blk", "dom", None, None),
        P("blk", "dom", None, None),
        P(),
        P("blk", None, None),
        P("blk", None, None),
        P("blk", "dom", None, None),
        P("blk", "dom", None, None),
        P("blk", "dom", None, None),
        P("blk", "dom", None),
        P("dom", "blk", None, None),
    )
    out_specs = (
        P("blk", "dom", None, None),
        P("blk", "dom", None, None),
        P("blk", "dom", None, None),
        P(),
        P(),
    )
    return jax.shard_map(
        on_device, mesh=mesh, in_specs=in_specs, out_specs=out_specs, check_vma=False
    )
```

profile of v0, /device:TPU:0, one launch (start us, length us, event | category | flops | bytes accessed | tf_op | source)
XLA Modules:
  0.0 304.0 jit_solution(15505422694455542022)
XLA Ops:
  7.2 0.8 broadcast_divide_fusion
  8.0 0.7 sign_compare_fusion
  9.3 0.3 convert_reduce_fusion.1
  9.8 0.4 convert_reduce_fusion
  10.2 1.4 convolution_convert_fusion.1
  11.6 1.1 copy.193
  12.7 7.3 %all-to-all-start = ((bf16[8,3,64,256]{3,2,1,0:T(8,128)(2,1)}), bf16[8,3,64,256]{3,2,1,0:T(8,128)(2,1)S(1)}, u32[]{:S(2)}, u32[]{:S(2)}) async-start(bf16[8,3,64,256]{3,2,1,0:T(8,128)(2,1)} %copy.193), calls=%async_computation | async-start | bytes 1572864 | tf_op jit(solution)/shard_map/all_to_all | solution.py:85
  20.0 0.2 dynamic-slice_reduce_fusion
  20.6 19.5 %all-to-all-done = bf16[8,3,64,256]{3,2,1,0:T(8,128)(2,1)S(1)} async-done(((bf16[8,3,64,256]{3,2,1,0:T(8,128)(2,1)}), bf16[8,3,64,256]{3,2,1,0:T(8,128)(2,1)S(1)}, u32[]{:S(2)}, u32[]{:S(2)}) %all-to-all-start) | async-done | bytes 786464 | tf_op jit(solution)/shard_map/all_to_all | solution.py:85
  40.1 0.5 fusion.3
  40.7 5.4 %fusion = bf16[2,64,1536]{2,1,0:T(8,128)(2,1)S(1)} fusion(bf16[2,6,256,1536]{3,2,1,0:T(8,128)(2,1)} %bitcast.139, bf16[2,6,64,256]{3,1,2,0:T(8,128)(2,1)S(1)} %fusion.3), kind=kOutput, calls=%fused_computation.5 | convolution fusion | flops 604176384 | bytes 10223616 | tf_op jit(solution)/shard_map/stcx,stxm->scm/dot_general | solution.py:10
  46.1 0.4 convert_element_type.71
  46.5 0.4 bitcast_convert_fusion.1
  46.9 0.2 copy.198
  47.1 23.8 %all_to_all.20 = bf16[8,3,64,256]{3,2,1,0:T(8,128)(2,1)S(1)} all-to-all(bf16[8,3,64,256]{3,2,1,0:T(8,128)(2,1)S(1)} %copy.198), channel_id=1, replica_groups=mesh['dom'=8,'blk'=4] {'dom'}, dimensions={0} | all-to-all | bytes 1572864 | tf_op jit(solution)/shard_map/all_to_all | solution.py:95
  70.9 0.9 fusion.20
  71.8 38.8 %psum.28 = f32[64]{0:T(128)S(1)} all-reduce(f32[64]{0:T(128)S(1)} %get-tuple-element.52), channel_id=1, replica_groups=mesh['dom'=8,'blk'=4] {'dom','blk'}, use_global_device_ids=true, to_apply=%region_3.4 | all-reduce | flops 64 | bytes 512 | tf_op jit(solution)/shard_map/psum | solution.py:102
  110.6 0.3 fusion.18
  110.9 0.4 convolution_convert_fusion
  111.3 1.1 copy.202
  112.4 4.9 %all-to-all-start.2 = ((bf16[8,3,64,256]{3,2,1,0:T(8,128)(2,1)}), bf16[8,3,64,256]{3,2,1,0:T(8,128)(2,1)}, u32[]{:S(2)}, u32[]{:S(2)}) async-start(bf16[8,3,64,256]{3,2,1,0:T(8,128)(2,1)} %copy.202), calls=%async_computation.2 | async-start | bytes 1572864 | tf_op jit(solution)/shard_map/all_to_all | solution.py:85
  117.4 1.6 copy.206
  119.0 17.5 %all-to-all-done.2 = bf16[8,3,64,256]{3,2,1,0:T(8,128)(2,1)} async-done(((bf16[8,3,64,256]{3,2,1,0:T(8,128)(2,1)}), bf16[8,3,64,256]{3,2,1,0:T(8,128)(2,1)}, u32[]{:S(2)}, u32[]{:S(2)}) %all-to-all-start.2) | async-done | bytes 786464 | tf_op jit(solution)/shard_map/all_to_all | solution.py:85
  136.5 1.7 convolution_bitcast_fusion.2
  138.2 1.8 convolution_bitcast_fusion.6
  140.0 0.1 copy.209
  140.1 3.5 %scatter_custom_fusion = f32[64,3072]{0,1:T(8,128)} fusion(s32[512]{0:T(512)S(1)} %bitcast.146, f32[512,64]{1,0:T(8,128)S(1)} %copy.209, f32[]{:T(128)} %constant.59.clone.1), kind=kCustom, calls=%fused_computation.28 | custom fusion | flops 32768 | bytes 786436 | tf_op jit(solution)/shard_map/scatter-add | solution.py:125
  143.6 2.4 convert_element_type.76
  146.0 6.3 %convolution_bitcast_fusion = f32[2,64,1536]{2,1,0:T(8,128)} fusion(bf16[2,6,256,1536]{3,2,1,0:T(8,128)(2,1)} %bitcast.140, bf16[2,6,64,256]{3,1,2,0:T(8,128)(2,1)S(1)} %convolution_bitcast_fusion.2), kind=kOutput, calls=%fused_computation.3 | convolution fusion | flops 603979776 | bytes 10616832 | tf_op jit(solution)/shard_map/stcx,stxm->scm/dot_general | solution.py:10
  152.3 16.6 %reduce-scatter.2.cloned.1.call-done = bf16[64,768]{0,1:T(8,128)(2,1)} async-done(((bf16[64,3072]{0,1:T(8,128)(2,1)}), bf16[64,768]{0,1:T(8,128)(2,1)}) %reduce-scatter.2.cloned.1.call-update) | async-done | bytes 98320 | tf_op jit(solution)/shard_map/reduce_scatter | solution.py:126
  168.9 1.3 fusion.6
  170.2 6.9 %all_gather.3 = bf16[64,3072]{1,0:T(8,128)(2,1)} all-gather(bf16[64,768]{1,0:T(8,128)(2,1)S(1)} %fusion.6), channel_id=1, replica_groups=mesh['dom'=8,'blk'=4] {'blk'}, dimensions={1}, use_global_device_ids=true | all-gather | bytes 491520 | tf_op jit(solution)/shard_map/all_gather | solution.py:132
  177.1 2.2 copy.210
  179.3 2.3 gather_fusion
  181.7 2.3 fusion.1
  183.9 1.4 convert_element_type.79
  185.4 0.4 bitcast_convert_fusion
  185.8 1.1 copy.213
  186.9 5.5 %all-to-all-start.3 = ((bf16[8,3,64,256]{3,2,1,0:T(8,128)(2,1)}), bf16[8,3,64,256]{3,2,1,0:T(8,128)(2,1)S(1)}, u32[]{:S(2)}, u32[]{:S(2)}) async-start(bf16[8,3,64,256]{3,2,1,0:T(8,128)(2,1)} %copy.213), calls=%async_computation.4 | async-start | bytes 1572864 | tf_op jit(solution)/shard_map/all_to_all | solution.py:95
  192.4 0.9 copy.217
  193.2 19.8 %all-to-all-done.3 = bf16[8,3,64,256]{3,2,1,0:T(8,128)(2,1)S(1)} async-done(((bf16[8,3,64,256]{3,2,1,0:T(8,128)(2,1)}), bf16[8,3,64,256]{3,2,1,0:T(8,128)(2,1)S(1)}, u32[]{:S(2)}, u32[]{:S(2)}) %all-to-all-start.3) | async-done | bytes 786464 | tf_op jit(solution)/shard_map/all_to_all | solution.py:95
  213.0 0.8 multiply_reduce_fusion.1
  213.8 37.9 %psum.29 = f32[64]{0:T(128)S(1)} all-reduce(f32[64]{0:T(128)S(1)} %get-tuple-element.54), channel_id=1, replica_groups=mesh['dom'=8,'blk'=4] {'dom','blk'}, use_global_device_ids=true, to_apply=%region_7.8 | all-reduce | flops 64 | bytes 512 | tf_op jit(solution)/shard_map/psum | solution.py:102
  251.7 2.1 multiply_reduce_fusion
  253.8 0.9 copy.215
  254.7 0.9 copy.216
  255.5 41.1 %all-reduce = (f32[64]{0:T(128)S(1)}, f32[64]{0:T(128)S(1)}) all-reduce(f32[64]{0:T(128)S(1)} %get-tuple-element.41, f32[64]{0:T(128)S(1)} %get-tuple-element.40), channel_id=1, replica_groups=mesh['dom'=8,'blk'=4] {'dom','blk'}, use_global_device_ids=true, to_apply=%region_11.12 | all-reduce | flops 128 | bytes 1024 | tf_op jit(solution)/shard_map/psum | solution.py:102
  296.6 0.5 multiply_divide_fusion
  (53 shorter events, 1.4 us)
Async XLA Ops:
  7.2 161.7 %copy-start = (bf16[1,1,768,768]{3,2,1,0:T(8,128)(2,1)S(1)}, bf16[1,1,768,768]{3,2,1,0:T(8,128)(2,1)}, u32[]{:S(2)}) copy-start(bf16[1,1,768,768]{3,2,1,0:T(8,128)(2,1)} %param.21) | copy-start | bytes 3538948
  11.6 8.7 %copy-start.7 = (s32[1,16,6]{1,0,2:T(1,128)S(1)}, s32[1,16,6]{1,0,2:T(1,128)}, u32[]{:S(2)}) copy-start(s32[1,16,6]{1,0,2:T(1,128)} %param.16) | copy-start | bytes 1156
  12.7 27.5 %all-to-all-start = ((bf16[8,3,64,256]{3,2,1,0:T(8,128)(2,1)}), bf16[8,3,64,256]{3,2,1,0:T(8,128)(2,1)S(1)}, u32[]{:S(2)}, u32[]{:S(2)}) async-start(bf16[8,3,64,256]{3,2,1,0:T(8,128)(2,1)} %copy.193), calls=%async_computation | async-start | bytes 1572864 | tf_op jit(solution)/shard_map/all_to_all | solution.py:85
  46.9 24.0 %copy-start.3 = (f32[1,6,64,256]{3,2,1,0:T(8,128)S(1)}, f32[1,6,64,256]{3,2,1,0:T(8,128)}, u32[]{:S(2)}) copy-start(f32[1,6,64,256]{3,2,1,0:T(8,128)} %param.12) | copy-start | bytes 1179652
  47.1 63.5 %copy-start.8 = (f32[64]{0:T(128)S(1)}, f32[64]{0:T(128)}, u32[]{:S(2)}) copy-start(f32[64]{0:T(128)} %param.14) | copy-start | bytes 772
  47.1 63.5 %copy-start.5 = (f32[1,6,64,256]{3,2,1,0:T(8,128)S(1)}, f32[1,6,64,256]{3,2,1,0:T(8,128)}, u32[]{:S(2)}) copy-start(f32[1,6,64,256]{3,2,1,0:T(8,128)} %param.13) | copy-start | bytes 1179652
  110.6 141.1 %copy-start.9 = (f32[64]{0:T(128)}, f32[64]{0:T(128)S(1)}, u32[]{:S(2)}) copy-start(f32[64]{0:T(128)S(1)} %get-tuple-element.45) | copy-start | bytes 772
  111.3 6.1 %copy-start.1 = (bf16[1,2,256,1536]{3,2,1,0:T(8,128)(2,1)S(1)}, bf16[1,2,256,1536]{3,2,1,0:T(8,128)(2,1)}, u32[]{:S(2)}) copy-start(bf16[1,2,256,1536]{3,2,1,0:T(8,128)(2,1)} %param.19) | copy-start | bytes 4718596
  112.4 24.1 %all-to-all-start.2 = ((bf16[8,3,64,256]{3,2,1,0:T(8,128)(2,1)}), bf16[8,3,64,256]{3,2,1,0:T(8,128)(2,1)}, u32[]{:S(2)}, u32[]{:S(2)}) async-start(bf16[8,3,64,256]{3,2,1,0:T(8,128)(2,1)} %copy.202), calls=%async_computation.2 | async-start | bytes 1572864 | tf_op jit(solution)/shard_map/all_to_all | solution.py:85
  117.3 1.7 copy-start.6
  117.3 51.5 %reduce-scatter.2.cloned.1.call-start = ((), (), s32[]{:S(2)}) async-start(), calls=%async_computation.5 | async-start | bytes 983040 | tf_op jit(solution)/shard_map/reduce_scatter | solution.py:126
  170.2 11.5 %copy-start.2 = (bf16[1,2,256,1536]{3,2,1,0:T(8,128)(2,1)S(1)}, bf16[1,2,256,1536]{3,2,1,0:T(8,128)(2,1)}, u32[]{:S(2)}) copy-start(bf16[1,2,256,1536]{3,2,1,0:T(8,128)(2,1)} %param.19) | copy-start | bytes 4718596
  186.9 26.2 %all-to-all-start.3 = ((bf16[8,3,64,256]{3,2,1,0:T(8,128)(2,1)}), bf16[8,3,64,256]{3,2,1,0:T(8,128)(2,1)S(1)}, u32[]{:S(2)}, u32[]{:S(2)}) async-start(bf16[8,3,64,256]{3,2,1,0:T(8,128)(2,1)} %copy.213), calls=%async_computation.4 | async-start | bytes 1572864 | tf_op jit(solution)/shard_map/all_to_all | solution.py:95
  192.4 59.3 %copy-start.4 = (f32[1,6,64,256]{3,2,1,0:T(8,128)S(1)}, f32[1,6,64,256]{3,2,1,0:T(8,128)}, u32[]{:S(2)}) copy-start(f32[1,6,64,256]{3,2,1,0:T(8,128)} %param.12) | copy-start | bytes 1179652
Sparse Core Ops, SparseCore 0:
  146.1 22.7 reduce-scatter.1
where the time goes:
time: 305 us; the launch traced here: 304 us
  blocking collectives  148 us (49%)
  waiting for transfers between devices  73.4 us (24%)
  matrix products  23.6 us (8%)
  starting transfers between devices  17.8 us (6%)
  local copies, waits for them, and re-layouts  15.4 us (5%)
  between operations  14.3 us (5%)
  other arithmetic  11 us (4%)
    psum x3, blocking collectives, global_sums(): return lax.psum(parts, ('dom', 'blk'))  118 us
    all_to_all x2, waiting for transfers between devices, fetch_multiply(): lax.all_to_all(outgoing, 'dom', split_axis=0, concat_axis=0, tiled=True)  37 us
    all_to_all x1, blocking collectives, return_sums(): lax.all_to_all(outgoing, 'dom', split_axis=0, concat_axis=0, tiled=True)  23.8 us
    all_to_all x1, waiting for transfers between devices, return_sums(): lax.all_to_all(outgoing, 'dom', split_axis=0, concat_axis=0, tiled=True)  19.8 us
    reduce_scatter x1, waiting for transfers between devices, on_device(): lax.psum_scatter(local_sums.astype(jnp.bfloat16), 'blk', scatter_dimensio...  16.6 us
    all_to_all x2, starting transfers between devices, fetch_multiply(): lax.all_to_all(outgoing, 'dom', split_axis=0, concat_axis=0, tiled=True)  12.2 us
    dot_general x2, matrix products, block_product(): jnp.einsum('stcx,stxm->scm', pieces, blocks, preferred_element_type=jnp.f...  11.7 us
    all_gather x1, blocking collectives, on_device(): everywhere = lax.all_gather(solved, 'blk', axis=1, tiled=True)  6.9 us
  transfers between devices with their start and end apart: 4, of which 4 were waited for; matrix products, arithmetic and copies ran while one was open for 3% of the time, Pallas kernels for 0%

commit v1 on v0

--- a/solution.py
+++ b/solution.py
@@ -1,7 +1,178 @@
+import functools
+
 import jax
 import jax.numpy as jnp
 from jax import lax
+from jax.experimental import pallas as pl
+from jax.experimental.pallas import tpu as pltpu
 from jax.sharding import PartitionSpec as P
+
+MESH = pl.DeviceIdType.MESH
+IN_VMEM = pl.BlockSpec(memory_space=pltpu.VMEM)
+
+
+def peers_of(axis):
+    count, me = lax.axis_size(axis), lax.axis_index(axis)
+    return [(k - 1, lax.rem(me + k, count)) for k in range(1, count)]
+
+
+def meet(axes):
+    barrier = pltpu.get_barrier_semaphore()
+    total = 0
+    for axis in axes:
+        for _, peer in peers_of(axis):
+            pl.semaphore_signal(barrier, inc=1, device_id={axis: peer}, device_id_type=MESH)
+            total += 1
+    pl.semaphore_wait(barrier, total)
+
+
+def remote(src, dst, send, recv, axis, peer):
+    return pltpu.make_async_remote_copy(
+        src_ref=src, dst_ref=dst, send_sem=send, recv_sem=recv,
+        device_id={axis: peer}, device_id_type=MESH,
+    )
+
+
+def sum_kernel(x_ref, o_ref, dom_slots, part, blk_slots, send_d, recv_d, send_b, recv_b):
+    meet(("dom", "blk"))
+    source = x_ref
+    for axis, slots, send, recv in (
+        ("dom", dom_slots, send_d, recv_d),
+        ("blk", blk_slots, send_b, recv_b),
+    ):
+        me = lax.axis_index(axis)
+        copies = [
+            remote(source, slots.at[me], send.at[k], recv.at[k], axis, peer)
+            for k, peer in peers_of(axis)
+        ]
+        for copy in copies:
+            copy.start()
+        slots[me] = source[...]
+        for copy in copies:
+            copy.wait()
+        total = slots[0]
+        for index in range(1, lax.axis_size(axis)):
+            total = total + slots[index]
+        if axis == "dom":
+            part[...] = total
+            source = part
+        else:
+            o_ref[...] = total
+
+
+def sum_everywhere(rows, collective_id):
+    case_count = rows[0].shape[0]
+    width = -(-case_count // 128) * 128
+    tile = jnp.pad(jnp.stack(rows), ((0, 8 - len(rows)), (0, width - case_count)))
+    n_dom, n_blk = lax.axis_size("dom"), lax.axis_size("blk")
+    dma = pltpu.SemaphoreType.DMA
+    sums = pl.pallas_call(
+        sum_kernel,
+        out_shape=jax.ShapeDtypeStruct(tile.shape, jnp.float32),
+        in_specs=[IN_VMEM],
+        out_specs=IN_VMEM,
+        scratch_shapes=[
+            pltpu.VMEM((n_dom,) + tile.shape, jnp.float32),
+            pltpu.VMEM(tile.shape, jnp.float32),
+            pltpu.VMEM((n_blk,) + tile.shape, jnp.float32),
+            dma((n_dom - 1,)), dma((n_dom - 1,)), dma((n_blk - 1,)), dma((n_blk - 1,)),
+        ],
+        compiler_params=pltpu.CompilerParams(collective_id=collective_id, has_side_effects=True),
+    )(tile)
+    return [sums[i, :case_count] for i in range(len(rows))]
+
+
+def exchange_kernel(x_ref, o_ref, send, recv, own):
+    meet(("dom",))
+    me = lax.axis_index("dom")
+    copies = [
+        remote(x_ref.at[peer], o_ref.at[me], send.at[k], recv.at[k], "dom", peer)
+        for k, peer in peers_of("dom")
+    ]
+    for copy in copies:
+        copy.start()
+    mine = pltpu.make_async_copy(x_ref.at[me], o_ref.at[me], own)
+    mine.start()
+    for copy in copies:
+        copy.wait()
+    mine.wait()
+
+
+def exchange(x, collective_id):
+    n_dom = lax.axis_size("dom")
+    dma = pltpu.SemaphoreType.DMA
+    return pl.pallas_call(
+        exchange_kernel,
+        out_shape=jax.ShapeDtypeStruct(x.shape, x.dtype),
+        in_specs=[IN_VMEM],
+        out_specs=IN_VMEM,
+        scratch_shapes=[dma((n_dom - 1,)), dma((n_dom - 1,)), dma],
+        compiler_params=pltpu.CompilerParams(collective_id=collective_id, has_side_effects=True),
+    )(x)
+
+
+def coarse_kernel(
+    terms_ref, ids_ref, inv_ref, o_ref, terms, ids, parts, picks,
+    send_t, recv_t, send_i, recv_i, send_p, recv_p,
+):
+    meet(("blk",))
+    n_blk, me = lax.axis_size("blk"), lax.axis_index("blk")
+    span = inv_ref.shape[0]
+    copies = []
+    for k, peer in peers_of("blk"):
+        copies.append(remote(ids_ref.at[peer], ids.at[me], send_i.at[k], recv_i.at[k], "blk", peer))
+        copies.append(remote(terms_ref.at[peer], terms.at[me], send_t.at[k], recv_t.at[k], "blk", peer))
+    for copy in copies:
+        copy.start()
+    terms[me] = terms_ref[me]
+    ids[me] = ids_ref[me]
+    for copy in copies:
+        copy.wait()
+
+    def hot(index):
+        rows = lax.broadcasted_iota(jnp.int32, (span, ids.shape[2]), 0)
+        return (rows == ids[index][:1, :]).astype(jnp.float32).astype(jnp.bfloat16)
+
+    rhs = jnp.zeros((terms.shape[1], span), jnp.float32)
+    for index in range(n_blk):
+        rhs += lax.dot_general(
+            terms[index], hot(index), (((1,), (1,)), ((), ())), preferred_element_type=jnp.float32
+        )
+    solved = jnp.dot(
+        rhs.astype(jnp.bfloat16), inv_ref[...], preferred_element_type=jnp.float32
+    ).astype(jnp.bfloat16)
+    for index in range(n_blk):
+        parts[index] = jnp.dot(
+            solved, hot(index), preferred_element_type=jnp.float32
+        ).astype(jnp.bfloat16)
+    copies = [
+        remote(parts.at[peer], picks.at[me], send_p.at[k], recv_p.at[k], "blk", peer)
+        for k, peer in peers_of("blk")
+    ]
+    for copy in copies:
+        copy.start()
+    picks[me] = parts[me]
+    for copy in copies:
+        copy.wait()
+    o_ref[...] = picks[...]
+
+
+def coarse_picks(terms, ids, inverse, collective_id):
+    n_blk = lax.axis_size("blk")
+    dma = pltpu.SemaphoreType.DMA
+    return pl.pallas_call(
+        coarse_kernel,
+        out_shape=jax.ShapeDtypeStruct(terms.shape, jnp.bfloat16),
+        in_specs=[IN_VMEM] * 3,
+        out_specs=IN_VMEM,
+        scratch_shapes=[
+            pltpu.VMEM(terms.shape, jnp.bfloat16),
+            pltpu.VMEM(ids.shape, jnp.int32),
+            pltpu.VMEM(terms.shape, jnp.bfloat16),
+            pltpu.VMEM(terms.shape, jnp.bfloat16),
+        ] + [dma((n_blk - 1,))] * 6,
+        compiler_params=pltpu.CompilerParams(collective_id=collective_id, has_side_effects=True),
+    )(terms, ids, inverse)
 
 
 def block_product(pieces, matrices):
@@ -68,7 +239,7 @@
         sub_count, face_slots, n_dom, capacity
     )
 
-    def fetch_multiply(vector_half, matrices, with_coarse):
+    def fetch_multiply(vector_half, matrices, with_coarse, collective_id):
 
         def finish(pieces):
             product = block_product(pieces, matrices)
@@ -82,64 +253,69 @@
         pieces = jnp.einsum(
             "stok,okcx->stcx",
             pull_table,
-            lax.all_to_all(outgoing, "dom", split_axis=0, concat_axis=0, tiled=True),
+            exchange(outgoing, collective_id),
             preferred_element_type=jnp.float32,
         ).astype(jnp.bfloat16)
         return finish(pieces)
 
-    def return_sums(totals):
+    def return_sums(totals, collective_id):
         per_slot = totals.reshape(sub_count, case_count, face_slots, face_len).astype(jnp.bfloat16)
         outgoing = jnp.einsum(
             "stok,sctx->okcx", pull_table, per_slot, preferred_element_type=jnp.float32
         ).astype(jnp.bfloat16)
-        incoming = lax.all_to_all(outgoing, "dom", split_axis=0, concat_axis=0, tiled=True)
+        incoming = exchange(outgoing, collective_id)
         summed = jnp.einsum(
             "dkf,dkcx->fcx", send_table, incoming, preferred_element_type=jnp.float32
         )
         return summed
 
-    def global_sums(parts):
-        return lax.psum(parts, ("dom", "blk"))
-
     total_count = n_dom * n_blk * faces_dev * face_len
     residual_rows = residual[0]
     precond_res = return_sums(
-        fetch_multiply(residual_rows.astype(jnp.bfloat16), dirichlet_blocks[0], False)
-    )
-    rho_sum, square_sum = global_sums(
+        fetch_multiply(residual_rows.astype(jnp.bfloat16), dirichlet_blocks[0], False, 0), 1
+    )
+    rho_sum, square_sum = sum_everywhere(
         (
             jnp.sum(residual_rows * precond_res, axis=(0, 2)),
             jnp.sum(residual_rows * residual_rows, axis=(0, 2)),
-        )
+        ),
+        2,
     )
     rho_now = rho_sum / total_count
     res_mean = square_sum / total_count
     beta_ratio = rho_now / rho_prev
     direction = precond_res + beta_ratio[None, :, None] * dir_prev[0]
-    product, corner_terms = fetch_multiply(direction.astype(jnp.bfloat16), dual_blocks[0], True)
+    product, corner_terms = fetch_multiply(direction.astype(jnp.bfloat16), dual_blocks[0], True, 3)
     corner_count = corner_terms.shape[2]
+    share = corner_count // n_blk
     block_span = coarse_inv.shape[2]
-    coarse_span = block_span * n_blk
-    flat_ids = corner_ids[0].reshape(-1)
-    values = jnp.transpose(corner_terms, (1, 0, 2)).reshape(case_count, sub_count * corner_count)
-    local_sums = jnp.zeros((case_count, coarse_span), jnp.float32).at[:, flat_ids].add(values)
-    owned_sums = lax.psum_scatter(
-        local_sums.astype(jnp.bfloat16), "blk", scatter_dimension=1, tiled=True
-    )
-    solved = jnp.dot(owned_sums, coarse_inv[0, 0], preferred_element_type=jnp.float32).astype(
-        jnp.bfloat16
-    )
-    everywhere = lax.all_gather(solved, "blk", axis=1, tiled=True)
-    picked = jnp.take(everywhere, flat_ids, axis=1).reshape(case_count, sub_count, corner_count)
+    by_block = jnp.transpose(
+        corner_terms.astype(jnp.bfloat16).reshape(sub_count, case_count, n_blk, share), (2, 1, 0, 3)
+    ).reshape(n_blk, case_count, sub_count * share)
+    block_ids = jnp.transpose(
+        (corner_ids[0] % block_span).reshape(sub_count, n_blk, share), (1, 0, 2)
+    ).reshape(n_blk, 1, sub_count * share)
+    block_ids = jnp.broadcast_to(block_ids, (n_blk, 8, sub_count * share))
+    picks = coarse_picks(by_block, block_ids, coarse_inv[0, 0], 4)
+    picked = jnp.transpose(
+        picks.reshape(n_blk, case_count, sub_count, share), (2, 1, 0, 3)
+    ).reshape(sub_count, case_count, corner_count)
     image_vec = return_sums(
         product
-        + jnp.einsum("csk,skl->scl", picked, coupling[0], preferred_element_type=jnp.float32)
-    )
-    curve_local = jnp.sum(direction * image_vec, axis=(0, 2))
-    (curve_sum,) = global_sums((curve_local,))
+        + jnp.einsum("sck,skl->scl", picked, coupling[0], preferred_element_type=jnp.float32),
+        5,
+    )
+    curve_sum, cross_sum, image_sum = sum_everywhere(
+        (
+            jnp.sum(direction * image_vec, axis=(0, 2)),
+            jnp.sum(residual_rows * image_vec, axis=(0, 2)),
+            jnp.sum(image_vec * image_vec, axis=(0, 2)),
+        ),
+        6,
+    )
     alpha_step = rho_now / (curve_sum / total_count)
     new_res = residual_rows - alpha_step[None, :, None] * image_vec
-    (new_sum,) = global_sums((jnp.sum(new_res * new_res, axis=(0, 2)),))
+    new_sum = square_sum - 2.0 * alpha_step * cross_sum + alpha_step * alpha_step * image_sum
     reduction = new_sum / total_count / res_mean
     new_lam = multipliers[0] + alpha_step[None, :, None] * direction
     return (new_lam[None], new_res[None], direction[None], rho_now, reduction)

time: 305 us -> 170 us (0.56)
  blocking collectives: 148 us -> 0 us
  Pallas kernels: 0 us -> 126 us
  waiting for transfers between devices: 73.4 us -> 0 us
  starting transfers between devices: 17.8 us -> 0 us
  between operations: 14.3 us -> 0.91 us
  other arithmetic: 11 us -> 6.2 us
    pallas_call x0 -> x7, Pallas kernels: none -> 126 us  [the longest x4 86 us: exchange(): pl.pallas_call(exchange_kernel, out_shape=jax.ShapeDtypeStruct(x.shape, x...]
    psum x3 -> x0, blocking collectives: 118 us -> none  [global_sums(): return lax.psum(parts, ('dom', 'blk'))]
    all_to_all x3 -> x0, waiting for transfers between devices: 56.8 us -> none  [the longest x2 37 us: fetch_multiply(): lax.all_to_all(outgoing, 'dom', split_axis=0, concat_axis=0, tiled=True)]
    all_to_all x1 -> x0, blocking collectives: 23.8 us -> none  [return_sums(): lax.all_to_all(outgoing, 'dom', split_axis=0, concat_axis=0, tiled=True)]
    all_to_all x3 -> x0, starting transfers between devices: 17.7 us -> none  [the longest x2 12.2 us: fetch_multiply(): lax.all_to_all(outgoing, 'dom', split_axis=0, concat_axis=0, tiled=True)]
    reduce_scatter x1 -> x0, waiting for transfers between devices: 16.6 us -> none  [on_device(): lax.psum_scatter(local_sums.astype(jnp.bfloat16), 'blk', scatter_dimensio...]
    all_gather x1 -> x0, blocking collectives: 6.9 us -> none  [on_device(): everywhere = lax.all_gather(solved, 'blk', axis=1, tiled=True)]
    dot_general x0 -> x4, local copies, waits for them, and re-layouts: none -> 4.21 us  [the longest x2 2.11 us: fetch_multiply(): jnp.einsum('dkf,fcx->dkcx', send_table, vector_half, preferred_element_ty...]
  transfers between devices with their start and end apart: 4 -> 0, of which waited for: 4 -> 0; matrix products, arithmetic and copies ran while one was open for 3% -> 0% of each run, Pallas kernels for 0% -> 0%
where the time goes in v1:
time: 170 us
  Pallas kernels  126 us (74%)
  matrix products  23.2 us (14%)
  local copies, waits for them, and re-layouts  13.6 us (8%)
  other arithmetic  6.2 us (4%)
    pallas_call x4, Pallas kernels, exchange(): pl.pallas_call(exchange_kernel, out_shape=jax.ShapeDtypeStruct(x.shape, x...  86 us
    pallas_call x2, Pallas kernels, sum_everywhere(): pl.pallas_call(sum_kernel, out_shape=jax.ShapeDtypeStruct(tile.shape, jnp...  30.6 us
    dot_general x2, matrix products, block_product(): jnp.einsum('stcx,stxm->scm', pieces, blocks, preferred_element_type=jnp.f...  10.8 us
    pallas_call x1, Pallas kernels, coarse_picks(): pl.pallas_call(coarse_kernel, out_shape=jax.ShapeDtypeStruct(terms.shape,...  9.08 us
    unnamed x21, local copies, waits for them, and re-layouts  4.31 us
    dot_general x2, matrix products, return_sums(): jnp.einsum('dkf,dkcx->fcx', send_table, incoming, preferred_element_type=...  4.27 us

profile of v1, /device:TPU:0, one launch (start us, length us, event | category | flops | bytes accessed | tf_op | source)
XLA Modules:
  0.0 169.6 jit_solution(1178743854103383399)
XLA Ops:
  0.6 0.7 broadcast_divide_fusion
  1.7 0.7 sign_compare_fusion
  2.3 0.1 copy.125
  2.6 0.3 convert_reduce_fusion.1
  3.0 0.2 dynamic-slice_reduce_fusion
  3.4 0.4 convert_reduce_fusion
  3.8 1.4 fusion.23
  5.2 1.1 copy.234.x_ref
  6.3 20.8 %shard_map.146 = bf16[8,3,64,256]{3,2,1,0:T(8,128)(2,1)} custom-call(bf16[8,3,64,256]{3,2,1,0:T(8,128)(2,1)} %copy.234.x_ref), custom_call_target="tpu_custom_call" | custom-call | tf_op jit(solution)/shard_map/pallas_call | solution.py:104
  27.5 1.7 fusion.3
  29.2 5.4 %fusion = bf16[2,64,1536]{2,1,0:T(8,128)(2,1)S(1)} fusion(bf16[2,6,256,1536]{3,2,1,0:T(8,128)(2,1)} %bitcast.158, bf16[2,6,64,256]{3,1,2,0:T(8,128)(2,1)S(1)} %fusion.3), kind=kOutput, calls=%fused_computation.3 | convolution fusion | flops 604176384 | bytes 10223616 | tf_op jit(solution)/shard_map/stcx,stxm->scm/dot_general | solution.py:181
  34.6 0.4 convert_element_type.72
  35.0 0.4 convolution_bitcast_fusion.3
  35.4 1.1 copy.233.x_ref
  36.5 22.6 %shard_map.147 = bf16[8,3,64,256]{3,2,1,0:T(8,128)(2,1)} custom-call(bf16[8,3,64,256]{3,2,1,0:T(8,128)(2,1)} %copy.233.x_ref), custom_call_target="tpu_custom_call" | custom-call | tf_op jit(solution)/shard_map/pallas_call | solution.py:104
  59.1 2.1 %fusion.14 = (f32[64]{0:T(128)S(1)}, f32[64]{0:T(128)S(1)}, f32[6,64,256]{2,0,1:T(8,128)S(1)}) fusion(f32[1,6,64,256]{3,2,1,0:T(8,128)S(1)} %copy-done, bf16[8,3,64,256]{3,2,1,0:T(8,128)(2,1)} %shard_map.147, bf16[8,3,6]{0,2,1:T(8,128)(2,1)S(1)} %convert_element_type.65), kind=kOutput, calls=%fused_computation.35 | convolution fusion | flops 5111680 | bytes 1573664 | tf_op jit(solution)/shard_map/dkf,dkcx->fcx/dot_general | solution.py:267
  61.2 0.6 select_maximum_fusion.2.x_ref
  61.8 15.3 %shard_map.148 = f32[8,128]{1,0:T(8,128)} custom-call(f32[8,128]{1,0:T(8,128)} %select_maximum_fusion.2.x_ref), custom_call_target="tpu_custom_call" | custom-call | tf_op jit(solution)/shard_map/pallas_call | solution.py:69
  77.1 0.7 fusion.53
  77.8 0.3 fusion.12
  78.0 0.4 fusion.25
  78.4 1.1 copy.232.x_ref
  79.5 19.1 %shard_map.149 = bf16[8,3,64,256]{3,2,1,0:T(8,128)(2,1)} custom-call(bf16[8,3,64,256]{3,2,1,0:T(8,128)(2,1)} %copy.232.x_ref), custom_call_target="tpu_custom_call" | custom-call | tf_op jit(solution)/shard_map/pallas_call | solution.py:104
  98.6 1.7 convolution_bitcast_fusion.4
  100.2 1.6 copy.145
  101.8 1.8 %fusion.4 = bf16[2,64,256]{2,1,0:T(8,128)(2,1)S(1)} fusion(bf16[2,256,6,256]{1,3,2,0:T(8,128)(2,1)} %bitcast.161, bf16[2,6,64,256]{3,1,2,0:T(8,128)(2,1)S(1)} %convolution_bitcast_fusion.4), kind=kOutput, calls=%fused_computation.18 | convolution fusion | flops 100696064 | bytes 2031616 | tf_op jit(solution)/shard_map/stcx,sktx->sck/dot_general | solution.py:187
  103.6 0.1 reshape.218
  103.7 0.1 copy.239
  103.9 0.7 reshape.219.terms_ref
  104.8 0.6 broadcast_in_dim.11.ids_ref
  105.4 9.1 %shard_map.150 = bf16[4,64,128]{2,1,0:T(8,128)(2,1)} custom-call(bf16[4,64,128]{2,1,0:T(8,128)(2,1)} %reshape.219.terms_ref, s32[4,8,128]{2,1,0:T(8,128)} %broadcast_in_dim.11.ids_ref, bf16[768,768]{1,0:T(8,128)(2,1)} %bitcast.162), custom_call_target="tpu_custom_call" | custom-call | tf_op jit(solution)/shard_map/pallas_call | solution.py:163
  114.5 0.9 reshape.220
  115.5 0.1 copy.149
  115.6 0.1 reshape.221
  115.7 5.4 %convolution_bitcast_fusion = f32[2,64,1536]{2,1,0:T(8,128)S(1)} fusion(bf16[2,6,256,1536]{3,2,1,0:T(8,128)(2,1)} %bitcast.159, bf16[2,6,64,256]{3,1,2,0:T(8,128)(2,1)S(1)} %convolution_bitcast_fusion.4), kind=kOutput, calls=%fused_computation.1 | convolution fusion | flops 603979776 | bytes 10616832 | tf_op jit(solution)/shard_map/stcx,stxm->scm/dot_general | solution.py:181
  121.1 0.4 fusion.1
  121.5 0.4 convert_element_type.79
  122.0 0.4 convolution_bitcast_fusion.2
  122.4 1.1 copy.231.x_ref
  123.4 23.5 %shard_map.151 = bf16[8,3,64,256]{3,2,1,0:T(8,128)(2,1)} custom-call(bf16[8,3,64,256]{3,2,1,0:T(8,128)(2,1)} %copy.231.x_ref), custom_call_target="tpu_custom_call" | custom-call | tf_op jit(solution)/shard_map/pallas_call | solution.py:104
  147.0 2.2 %multiply_reduce_fusion.1 = (f32[64]{0:T(128)S(1)}, f32[64]{0:T(128)S(1)}, f32[64]{0:T(128)S(1)}, f32[6,64,256]{2,0,1:T(8,128)S(1)}) fusion(f32[6,64,256]{2,0,1:T(8,128)S(1)} %fusion.12, f32[1,6,64,256]{3,2,1,0:T(8,128)S(1)} %copy-done, bf16[8,3,64,256]{3,2,1,0:T(8,128)(2,1)} %shard_map.151, bf16[8,3,6]{0,2,1:T(8,128)(2,1)S(1)} %convert_element_type.65), kind=kOutput, calls=%fused_computation.44 | convolution fusion | flops 5308224 | bytes 1967136 | tf_op jit(solution)/shard_map/dkf,dkcx->fcx/dot_general | solution.py:267
  149.2 0.6 select_maximum_fusion.x_ref
  149.8 15.3 %shard_map.152 = f32[8,128]{1,0:T(8,128)} custom-call(f32[8,128]{1,0:T(8,128)} %select_maximum_fusion.x_ref), custom_call_target="tpu_custom_call" | custom-call | tf_op jit(solution)/shard_map/pallas_call | solution.py:69
  165.1 1.3 fusion.49
  166.5 0.5 fusion.17
  167.0 0.9 copy.153
  167.8 0.9 copy.154
  168.7 0.9 copy.155
  (43 shorter events, 1.3 us)
Async XLA Ops:
  5.2 22.0 %copy-start.4 = (s32[1,16,6]{1,0,2:T(1,128)S(1)}, s32[1,16,6]{1,0,2:T(1,128)}, u32[]{:S(2)}) copy-start(s32[1,16,6]{1,0,2:T(1,128)} %param.16) | copy-start | bytes 1156
  35.4 23.7 %copy-start = (f32[1,6,64,256]{3,2,1,0:T(8,128)S(1)}, f32[1,6,64,256]{3,2,1,0:T(8,128)}, u32[]{:S(2)}) copy-start(f32[1,6,64,256]{3,2,1,0:T(8,128)} %param.12) | copy-start | bytes 1179652
  36.5 40.6 %copy-start.7 = (f32[64]{0:T(128)S(1)}, f32[64]{0:T(128)}, u32[]{:S(2)}) copy-start(f32[64]{0:T(128)} %param.14) | copy-start | bytes 772
  36.5 41.3 %copy-start.3 = (f32[1,6,64,256]{3,2,1,0:T(8,128)S(1)}, f32[1,6,64,256]{3,2,1,0:T(8,128)}, u32[]{:S(2)}) copy-start(f32[1,6,64,256]{3,2,1,0:T(8,128)} %param.13) | copy-start | bytes 1179652
  77.8 87.4 %copy-start.6 = (f32[64]{0:T(128)}, f32[64]{0:T(128)S(1)}, u32[]{:S(2)}) copy-start(f32[64]{0:T(128)S(1)} %get-tuple-element.38) | copy-start | bytes 772
  79.5 20.7 %copy-start.1 = (bf16[1,2,256,1536]{3,2,1,0:T(8,128)(2,1)S(1)}, bf16[1,2,256,1536]{3,2,1,0:T(8,128)(2,1)}, u32[]{:S(2)}) copy-start(bf16[1,2,256,1536]{3,2,1,0:T(8,128)(2,1)} %param.19) | copy-start | bytes 4718596
  101.8 2.8 %copy-start.5 = (s32[1,2,256]{2,1,0:T(2,128)S(1)}, s32[1,2,256]{2,1,0:T(2,128)}, u32[]{:S(2)}) copy-start(s32[1,2,256]{2,1,0:T(2,128)} %param.20) | copy-start | bytes 6148
  147.0 19.5 %copy-start.2 = (f32[1,6,64,256]{3,2,1,0:T(8,128)S(1)}, f32[1,6,64,256]{3,2,1,0:T(8,128)}, u32[]{:S(2)}) copy-start(f32[1,6,64,256]{3,2,1,0:T(8,128)} %param.11) | copy-start | bytes 1179652

commit v2 on v0

v2 whole, which is shorter than its diff:
```python
import jax
import jax.numpy as jnp
from jax import lax
from jax.experimental import pallas as pl
from jax.experimental.pallas import tpu as pltpu
from jax.sharding import PartitionSpec as P

MESH = pl.DeviceIdType.MESH
F32, BF16 = jnp.float32, jnp.bfloat16


def peers_of(axis):
    count, me = lax.axis_size(axis), lax.axis_index(axis)
    return [(k - 1, lax.rem(me + k, count)) for k in range(1, count)]


def remote(src, dst, send, recv, axis, peer):
    return pltpu.make_async_remote_copy(
        src_ref=src, dst_ref=dst, send_sem=send, recv_sem=recv,
        device_id={axis: peer}, device_id_type=MESH,
    )


def step_kernel(
    send_face, pull_slot, push_slot, first, second, sign,
    lam_ref, res_ref, dir_ref, rho_ref, ids_ref,
    dirichlet, dual, coupling, inverse,
    new_lam, new_res, new_dir, stats,
    w_dir, w_dual, w_cpl, w_inv, outs, in_0, in_1, in_2, in_3, slots, per_slot, image,
    dom_sums, part, blk_sums, ids, terms_out, terms_in, picks_out, picks_in,
    load, send_x, recv_x, send_s, recv_s, send_t, recv_t, send_c, recv_c,
):
    n_dom, n_blk = lax.axis_size("dom"), lax.axis_size("blk")
    me, my_blk = lax.axis_index("dom"), lax.axis_index("blk")
    faces, cases, face_len = res_ref.shape
    subs = slots.shape[0]
    fps = slots.shape[2] // face_len
    cap = send_face.shape[0] // n_dom
    count = n_dom * n_blk * faces * face_len
    share = ids.shape[3]
    ins = (in_0, in_1, in_2, in_3)
    span = w_inv.shape[0]

    loads = [
        pltpu.make_async_copy(src, dst, load.at[i])
        for i, (src, dst) in enumerate(
            ((dirichlet, w_dir), (coupling, w_cpl), (dual, w_dual), (inverse, w_inv))
        )
    ]
    for copy in loads:
        copy.start()

    barrier = pltpu.get_barrier_semaphore()
    for axis in ("dom", "blk"):
        for _, peer in peers_of(axis):
            pl.semaphore_signal(barrier, inc=1, device_id={axis: peer}, device_id_type=MESH)
    pl.semaphore_wait(barrier, n_dom + n_blk - 2)

    def exchange(turn, value_at):
        copies = []
        for k, peer in peers_of("dom"):
            for place in range(cap):
                outs[turn, peer * cap + place] = value_at(peer * cap + place)
            copy = remote(
                outs.at[turn, pl.ds(peer * cap, cap)], ins[turn].at[pl.ds(me * cap, cap)],
                send_x.at[turn, k], recv_x.at[turn, k], "dom", peer,
            )
            copy.start()
            copies.append(copy)
        for place in range(cap):
            ins[turn][me * cap + place] = value_at(me * cap + place)
        return copies

    def finish(copies):
        for copy in copies:
            copy.wait()

    def pull(turn, vector):
        return exchange(turn, lambda i: vector[send_face[i]].astype(BF16))

    def to_slots(turn):
        for s in range(subs):
            for t in range(fps):
                i = s * fps + t
                value = ins[turn][pull_slot[i]].astype(F32) * sign[i]
                slots[s, :, t * face_len:(t + 1) * face_len] = value.astype(BF16)

    def product(weights, s, t):
        return jnp.dot(
            slots[s], weights[s, :, t * face_len:(t + 1) * face_len], preferred_element_type=F32
        )

    def push(turn):
        return exchange(turn, lambda i: per_slot[push_slot[i]])

    def face_sum(turn, f):
        return ins[turn][first[f]].astype(F32) + ins[turn][second[f]].astype(F32)

    def as_rows(columns):
        lanes = part.shape[2]
        place = lax.broadcasted_iota(jnp.int32, (cases, 128), 1)
        tile = jnp.zeros((cases, 128), F32)
        for i, column in enumerate(columns):
            tile = jnp.where(place == i, column, tile)
        if lanes > cases:
            tile = jnp.concatenate([tile, jnp.zeros((lanes - cases, 128), F32)], axis=0)
        return jnp.transpose(tile)[:8]

    def as_column(row):
        tile = jnp.concatenate([row, jnp.zeros((127, row.shape[1]), F32)], axis=0)
        return jnp.transpose(tile)[:cases, :1]

    def total_of(turn, columns):
        part[2 * turn] = as_rows(columns)
        for level, axis, sums, base in (
            (0, "dom", dom_sums, 0), (1, "blk", blk_sums, n_dom - 1),
        ):
            here = lax.axis_index(axis)
            source = 2 * turn + level
            copies = [
                remote(
                    part.at[source], sums.at[turn, here],
                    send_s.at[turn, base + k], recv_s.at[turn, base + k], axis, peer,
                )
                for k, peer in peers_of(axis)
            ]
            for copy in copies:
                copy.start()
            sums[turn, here] = part[source]
            finish(copies)
            total = sums[turn, 0]
            for index in range(1, lax.axis_size(axis)):
                total = total + sums[turn, index]
            if level == 0:
                part[source + 1] = total
        return total

    def lane_sum(value):
        return jnp.sum(value, axis=1, keepdims=True)

    pulled = pull(0, res_ref)
    id_copies = [
        remote(ids_ref.at[peer], ids.at[my_blk], send_c.at[0, k], recv_c.at[0, k], "blk", peer)
        for k, peer in peers_of("blk")
    ]
    for copy in id_copies:
        copy.start()
    ids[my_blk] = ids_ref[my_blk]
    square = jnp.zeros((cases, face_len), F32)
    for f in range(faces):
        square += res_ref[f] * res_ref[f]
    loads[0].wait()
    finish(pulled)
    to_slots(0)
    for s in range(subs):
        for t in range(fps):
            i = s * fps + t
            per_slot[i] = (product(w_dir, s, t) * sign[i]).astype(BF16)
    finish(push(1))
    rho_part = jnp.zeros((cases, face_len), F32)
    for f in range(faces):
        value = face_sum(1, f)
        image[f] = value
        rho_part += res_ref[f] * value
    first_total = total_of(0, (lane_sum(rho_part), lane_sum(square)))
    rho_now = first_total[0:1] / count
    square_sum = first_total[1:2]
    beta = as_column(rho_now / rho_ref[0:1])
    for f in range(faces):
        new_dir[f] = image[f] + beta * dir_ref[f]

    pulled = pull(2, new_dir)
    loads[1].wait()
    loads[2].wait()
    loads[3].wait()
    finish(id_copies)
    finish(pulled)
    to_slots(2)
    for b in range(n_blk):
        for s in range(subs):
            terms_out[b, s] = lax.dot_general(
                slots[s], w_cpl[s, b * share:(b + 1) * share, :], (((1,), (1,)), ((), ())),
                preferred_element_type=F32,
            ).astype(BF16)
    copies = [
        remote(terms_out.at[peer], terms_in.at[my_blk], send_t.at[0, k], recv_t.at[0, k], "blk", peer)
        for k, peer in peers_of("blk")
    ]
    for copy in copies:
        copy.start()
    terms_in[my_blk] = terms_out[my_blk]
    sums = [[product(w_dual, s, t) for t in range(fps)] for s in range(subs)]
    finish(copies)

    def hot(p, s):
        rows = lax.broadcasted_iota(jnp.int32, (span, share), 0)
        return (rows == ids[p, s][:1, :]).astype(F32).astype(BF16)

    rhs = jnp.zeros((cases, span), F32)
    for p in range(n_blk):
        for s in range(subs):
            rhs += lax.dot_general(
                terms_in[p, s], hot(p, s), (((1,), (1,)), ((), ())), preferred_element_type=F32
            )
    solved = jnp.dot(rhs.astype(BF16), w_inv[...], preferred_element_type=F32).astype(BF16)
    for p in range(n_blk):
        for s in range(subs):
            picks_out[p, s] = jnp.dot(solved, hot(p, s), preferred_element_type=F32).astype(BF16)
    copies = [
        remote(picks_out.at[peer], picks_in.at[my_blk], send_t.at[1, k], recv_t.at[1, k], "blk", peer)
        for k, peer in peers_of("blk")
    ]
    for copy in copies:
        copy.start()
    picks_in[my_blk] = picks_out[my_blk]
    finish(copies)
    for s in range(subs):
        for t in range(fps):
            i = s * fps + t
            value = sums[s][t]
            for b in range(n_blk):
                value += jnp.dot(
                    picks_in[b, s],
                    w_cpl[s, b * share:(b + 1) * share, t * face_len:(t + 1) * face_len],
                    preferred_element_type=F32,
                )
            per_slot[i] = (value * sign[i]).astype(BF16)
    finish(push(3))
    curve = jnp.zeros((cases, face_len), F32)
    cross = jnp.zeros((cases, face_len), F32)
    norm = jnp.zeros((cases, face_len), F32)
    for f in range(faces):
        value = face_sum(3, f)
        image[f] = value
        curve += new_dir[f] * value
        cross += res_ref[f] * value
        norm += value * value
    last_total = total_of(1, (lane_sum(curve), lane_sum(cross), lane_sum(norm)))
    alpha = rho_now / (last_total[0:1] / count)
    new_sum = square_sum - 2.0 * alpha * last_total[1:2] + alpha * alpha * last_total[2:3]
    stats[0:1] = rho_now
    stats[1:2] = (new_sum / count) / (square_sum / count)
    stats[2:8] = jnp.zeros((6, stats.shape[1]), F32)
    step = as_column(alpha)
    for f in range(faces):
        new_lam[f] = lam_ref[f] + step * new_dir[f]
        new_res[f] = res_ref[f] - step * image[f]


def on_device(
    multipliers, residual, dir_prev, rho_prev, face_ids, face_sign,
    dual_blocks, dirichlet_blocks, coupling, corner_ids, coarse_inv,
):
    n_dom, n_blk = lax.axis_size("dom"), lax.axis_size("blk")
    me = lax.axis_index("dom")
    _, faces, cases, face_len = multipliers.shape
    _, subs, local, _ = dual_blocks.shape
    slot_count = subs * face_ids.shape[2]
    column_ids = face_ids[0].reshape(n_dom, slot_count)
    signs = face_sign[0].reshape(n_dom, slot_count)
    cap = (slot_count + n_dom - 1) // n_dom + 1
    owners = column_ids // faces
    order = jnp.arange(slot_count)
    earlier = (owners[:, :, None] == owners[:, None, :]) & (order[None, None, :] < order[None, :, None])
    rank = jnp.sum(earlier.astype(jnp.int32), axis=2)
    places = jnp.arange(cap)
    mine = ((owners == me)[:, :, None]) & (rank[:, :, None] == places)
    send_face = jnp.sum(jnp.where(mine, (column_ids % faces)[:, :, None], 0), axis=1).reshape(-1)
    code = jnp.arange(n_dom)[:, None] * cap + rank
    match = (column_ids - me * faces)[:, :, None] == jnp.arange(faces)
    first = jnp.min(jnp.where(match, code[:, :, None], n_dom * cap - 1), axis=(0, 1))
    second = jnp.max(jnp.where(match, code[:, :, None], 0), axis=(0, 1))
    my_owner = lax.dynamic_index_in_dim(owners, me, 0, keepdims=False)
    my_rank = lax.dynamic_index_in_dim(rank, me, 0, keepdims=False)
    my_sign = lax.dynamic_index_in_dim(signs, me, 0, keepdims=False).astype(F32)
    pull_slot = my_owner * cap + my_rank
    push_slot = jnp.sum(
        jnp.where(pull_slot[None, :] == jnp.arange(n_dom * cap)[:, None], order[None, :], 0), axis=1
    )
    span = coarse_inv.shape[2]
    corners = coupling.shape[2]
    share = corners // n_blk
    block_ids = jnp.transpose((corner_ids[0] % span).reshape(subs, n_blk, share), (1, 0, 2))
    block_ids = jnp.broadcast_to(block_ids[:, :, None, :], (n_blk, subs, 8, share))
    lanes = -(-cases // 128) * 128
    rho_tile = jnp.broadcast_to(
        jnp.pad(rho_prev, (0, lanes - cases), constant_values=1.0)[None, :], (8, lanes)
    )
    field = jax.ShapeDtypeStruct((faces, cases, face_len), F32)
    vmem = pl.BlockSpec(memory_space=pltpu.VMEM)
    smem = pl.BlockSpec(memory_space=pltpu.SMEM)
    hbm = pl.BlockSpec(memory_space=pl.ANY)
    dma = pltpu.SemaphoreType.DMA
    dom_peers, blk_peers = n_dom - 1, n_blk - 1
    terms = pltpu.VMEM((n_blk, subs, cases, share), BF16)
    piece = (n_dom * cap, cases, face_len)
    new_lam, new_res, new_dir, stats = pl.pallas_call(
        step_kernel,
        out_shape=(field, field, field, jax.ShapeDtypeStruct((8, lanes), F32)),
        in_specs=[smem] * 6 + [vmem] * 5 + [hbm] * 4,
        out_specs=(vmem,) * 4,
        scratch_shapes=[
            pltpu.VMEM((subs, local, local), BF16),
            pltpu.VMEM((subs, local, local), BF16),
            pltpu.VMEM((subs, corners, local), BF16),
            pltpu.VMEM((span, span), BF16),
            pltpu.VMEM((4,) + piece, BF16),
            *[pltpu.VMEM(piece, BF16)] * 4,
            pltpu.VMEM((subs, cases, local), BF16),
            pltpu.VMEM((slot_count, cases, face_len), BF16),
            pltpu.VMEM((faces, cases, face_len), F32),
            pltpu.VMEM((2, n_dom, 8, lanes), F32),
            pltpu.VMEM((4, 8, lanes), F32),
            pltpu.VMEM((2, n_blk, 8, lanes), F32),
            pltpu.VMEM((n_blk, subs, 8, share), jnp.int32),
            terms, terms, terms, terms,
            dma((4,)),
            dma((4, dom_peers)), dma((4, dom_peers)),
            dma((2, dom_peers + blk_peers)), dma((2, dom_peers + blk_peers)),
            dma((2, blk_peers)), dma((2, blk_peers)),
            dma((1, blk_peers)), dma((1, blk_peers)),
        ],
        compiler_params=pltpu.CompilerParams(
            collective_id=0, has_side_effects=True, vmem_limit_bytes=60 << 20
        ),
    )(
        send_face, pull_slot, push_slot, first, second, my_sign,
        multipliers[0], residual[0], dir_prev[0], rho_tile, block_ids,
        dirichlet_blocks[0], dual_blocks[0], coupling[0], coarse_inv[0, 0],
    )
    return new_lam[None], new_res[None], new_dir[None], stats[0, :cases], stats[1, :cases]


def solution(mesh):
    in_specs = (
        P("blk", "dom", None, None),
        P("blk", "dom", None, None),
        P("blk", "dom", None, None),
        P(),
        P("blk", None, None),
        P("blk", None, None),
        P("blk", "dom", None, None),
        P("blk", "dom", None, None),
        P("blk", "dom", None, None),
        P("blk", "dom", None),
        P("dom", "blk", None, None),
    )
    out_specs = (
        P("blk", "dom", None, None),
        P("blk", "dom", None, None),
        P("blk", "dom", None, None),
        P(),
        P(),
    )
    return jax.shard_map(
        on_device, mesh=mesh, in_specs=in_specs, out_specs=out_specs, check_vma=False
    )
```

time: 305 us -> 127 us (0.42)
  blocking collectives: 148 us -> 0 us
  Pallas kernels: 0 us -> 111 us
  waiting for transfers between devices: 73.4 us -> 0 us
  matrix products: 23.6 us -> 0 us
  starting transfers between devices: 17.8 us -> 0 us
  between operations: 14.3 us -> 0.67 us
  other arithmetic: 11 us -> 4.68 us
  local copies, waits for them, and re-layouts: 15.4 us -> 10.9 us
    psum x3 -> x0, blocking collectives: 118 us -> none  [global_sums(): return lax.psum(parts, ('dom', 'blk'))]
    pallas_call x0 -> x1, Pallas kernels: none -> 111 us  [on_device(): pl.pallas_call(step_kernel, out_shape=(field, field, field, jax.ShapeDtyp...]
    all_to_all x3 -> x0, waiting for transfers between devices: 56.8 us -> none  [the longest x2 37 us: fetch_multiply(): lax.all_to_all(outgoing, 'dom', split_axis=0, concat_axis=0, tiled=True)]
    all_to_all x1 -> x0, blocking collectives: 23.8 us -> none  [return_sums(): lax.all_to_all(outgoing, 'dom', split_axis=0, concat_axis=0, tiled=True)]
    dot_general x13 -> x0, matrix products: 23.6 us -> none  [the longest x2 11.7 us: block_product(): jnp.einsum('stcx,stxm->scm', pieces, blocks, preferred_element_type=jnp.f...]
    all_to_all x3 -> x0, starting transfers between devices: 17.7 us -> none  [the longest x2 12.2 us: fetch_multiply(): lax.all_to_all(outgoing, 'dom', split_axis=0, concat_axis=0, tiled=True)]
    reduce_scatter x1 -> x0, waiting for transfers between devices: 16.6 us -> none  [on_device(): lax.psum_scatter(local_sums.astype(jnp.bfloat16), 'blk', scatter_dimensio...]
    all_gather x1 -> x0, blocking collectives: 6.9 us -> none  [on_device(): everywhere = lax.all_gather(solved, 'blk', axis=1, tiled=True)]
  transfers between devices with their start and end apart: 4 -> 0, of which waited for: 4 -> 0; matrix products, arithmetic and copies ran while one was open for 3% -> 0% of each run, Pallas kernels for 0% -> 0%
where the time goes in v2:
time: 127 us
  Pallas kernels  111 us (87%)
  local copies, waits for them, and re-layouts  10.9 us (9%)
  other arithmetic  4.68 us (4%)
    pallas_call x1, Pallas kernels, on_device(): pl.pallas_call(step_kernel, out_shape=(field, field, field, jax.ShapeDtyp...  111 us
    unnamed x6, local copies, waits for them, and re-layouts  6.09 us

profile of v2, /device:TPU:0, one launch (start us, length us, event | category | flops | bytes accessed | tf_op | source)
XLA Modules:
  0.0 126.9 jit_solution(13088190560520884024)
XLA Ops:
  0.6 0.7 pad.4
  1.3 0.7 broadcast_remainder_fusion.1
  2.0 0.1 rem.51
  2.1 0.7 sign_compare_fusion
  2.8 0.1 copy.78
  2.9 0.1 ne.66
  3.0 0.6 broadcast_in_dim.86.rho_ref
  3.6 0.8 copy.87
  4.3 0.1 reshape_squeeze.4
  4.4 0.7 broadcast_subtract_fusion
  5.1 0.1 copy.85
  5.2 0.1 sub.22
  5.3 0.1 copy.79
  5.3 0.1 rem.47
  5.4 0.1 copy.80
  5.5 0.1 div.21
  5.6 0.1 copy.81
  5.7 0.3 convert_reduce_fusion
  6.0 0.1 copy.82
  6.1 0.5 fusion.5
  6.6 0.0 copy-start
  6.6 0.1 select_reduce_fusion.2
  6.8 0.1 broadcast_add_fusion
  6.9 0.9 select_reduce_fusion
  7.7 0.6 select_reduce_fusion.3.push_slot
  8.3 0.1 copy.83
  8.4 0.6 reshape.126.send_face
  9.0 0.6 broadcast_in_dim.87.ids_ref
  9.6 0.0 copy-done
  9.6 110.6 %shard_map.146 = (f32[6,64,256]{2,1,0:T(8,128)}, f32[6,64,256]{2,1,0:T(8,128)}, f32[6,64,256]{2,1,0:T(8,128)}, f32[8,128]{1,0:T(8,128)}) custom-call(s32[24]{0:T(128)} %reshape.126.send_face, s32[12]{0:T(128)} %copy-done, s32[24]{0:T(128)} %select_reduce_fusion.3.push_slot, s32[6]{0:T(128)} %get-tuple-element.14.first, s32[6]{0:T(128)} %get-tuple-element.13.second, ...), custom_call_target="tpu_custom_call" | custom-call | tf_op jit(solution)/shard_map/pallas_call | solution.py:297
  120.3 1.3 slice_bitcast_fusion
  121.5 1.8 %copy.96 = f32[1,6,64,256]{3,2,1,0:T(8,128)} copy(f32[1,6,64,256]{3,2,1,0:T(8,128)} %bitcast.26) | data formatting | bytes 786432
  123.3 1.8 %copy.97 = f32[1,6,64,256]{3,2,1,0:T(8,128)} copy(f32[1,6,64,256]{3,2,1,0:T(8,128)} %bitcast.25) | data formatting | bytes 786432
  125.1 1.8 %copy.98 = f32[1,6,64,256]{3,2,1,0:T(8,128)} copy(f32[1,6,64,256]{3,2,1,0:T(8,128)} %bitcast.24) | data formatting | bytes 786432
  (5 shorter events, 0.0 us)
Async XLA Ops:
  6.6 3.0 %copy-start = (s32[12]{0:T(128)}, s32[12]{0:T(128)S(1)}, u32[]{:S(2)}) copy-start(s32[12]{0:T(128)S(1)} %get-tuple-element.23.pull_slot) | copy-start | bytes 148
